TPU v7x, 32 devices: a whole 2x2x4 slice. The times are simulated.
32 devices in a mesh: blk: 8 (over z, core), seq: 4 (over y, x).
Axes of the slice: x: 2, y: 2, z: 4, core: 2. Of those that a mesh axis runs over, the one named last changes fastest.
Arguments:
- activations: bfloat16 [8, 2048, 8192], P('blk', 'seq'), may hold values from -6 to 6
- base_weight: bfloat16 [8192, 1024], P('blk', 'seq'), may hold values from -0.0625 to 0.0625
- adapter_down: bfloat16 [8, 16, 8192], P('blk'), may hold values from -0.0625 to 0.0625
- adapter_up: bfloat16 [8, 16, 1024], P('blk'), may hold values from -1.5 to 1.5
- cotangent: bfloat16 [8, 2048, 1024], P('blk', 'seq'), may hold values from -12 to 12
Outputs:
- projected: bfloat16 [8, 2048, 1024], P('blk', 'seq')
- gradient_inputs: bfloat16 [8, 2048, 8192], P('blk', 'seq')
- down_gradient: float32 [8, 16, 8192], P('blk')
- up_gradient: float32 [8, 16, 1024], P('blk')
All inputs are finite; a program needn't handle non-finite values.
Results may differ from a plain program's by a relative error of at most 0.0047.
Values may be sent and summed in bfloat16 or wider, within the bound.
No kernel may reach another device: no remote copies, remote signals or barrier semaphores. Data moves between devices by JAX's collectives and lax.ppermute only.
A program may use at most 128 MiB of HBM per device.

v0:
```python
import jax
import jax.numpy as jnp
from jax import lax
from jax.sharding import PartitionSpec as P

adapter_scale = 2.0


def body(activations, base_weight, adapter_down, adapter_up, cotangent):
    token_inputs = activations[0]
    down_matrix = adapter_down[0]
    up_matrix = adapter_up[0]
    output_cotangent = cotangent[0]
    token_count = token_inputs.shape[0] * lax.axis_size("seq")
    panel = lax.all_gather(base_weight, "seq", axis=1, tiled=True)
    lowrank_forward = jnp.dot(
        token_inputs, down_matrix.T, preferred_element_type=jnp.float32
    ).astype(jnp.bfloat16)
    lowrank_backward = jnp.dot(
        output_cotangent, up_matrix.T, preferred_element_type=jnp.float32
    ).astype(jnp.bfloat16)
    frozen_keys = jnp.dot(
        token_inputs,
        lax.all_gather(panel, "blk", axis=0, tiled=True),
        preferred_element_type=jnp.float32,
    )
    frozen_gradient = lax.dot_general(
        output_cotangent,
        lax.all_gather(panel, "blk", axis=0, tiled=True),
        (((1,), (1,)), ((), ())),
        preferred_element_type=jnp.float32,
    )
    projected = frozen_keys + adapter_scale * jnp.dot(
        lowrank_forward, up_matrix, preferred_element_type=jnp.float32
    )
    gradient_inputs = frozen_gradient + adapter_scale * jnp.dot(
        lowrank_backward, down_matrix, preferred_element_type=jnp.float32
    )
    local_down = jnp.dot(lowrank_backward.T, token_inputs, preferred_element_type=jnp.float32)
    local_up = jnp.dot(lowrank_forward.T, output_cotangent, preferred_element_type=jnp.float32)
    sum_down, sum_up = lax.psum((local_down, local_up), "seq")
    scale_factor = adapter_scale / token_count
    return (
        projected.astype(jnp.bfloat16)[None],
        gradient_inputs.astype(jnp.bfloat16)[None],
        (scale_factor * sum_down)[None],
        (scale_factor * sum_up)[None],
    )


def solution(mesh):
    return jax.shard_map(
        body,
        mesh=mesh,
        in_specs=(
            P("blk", "seq", None),
            P("blk", "seq"),
            P("blk", None, None),
            P("blk", None, None),
            P("blk", "seq", None),
        ),
        out_specs=(
            P("blk", "seq", None),
            P("blk", "seq", None),
            P("blk", None, None),
            P("blk", None, None),
        ),
        check_vma=False,
    )
```

profile of v0, /device:TPU:0, one launch (start us, length us, event | category | flops | bytes accessed | tf_op | source)
XLA Modules:
  0.0 299.8 jit_solution(208566958700023274)
XLA Ops:
  7.2 0.0 copy-start
  7.2 0.0 all-gather.3.cloned.1.call-start
  7.2 0.7 all-gather.3.cloned.1.call-update
  7.9 0.0 all-reduce.3.cloned.1.call-start
  8.0 0.4 copy-done
  8.4 0.0 copy-start.1
  8.4 1.3 convolution_convert_fusion
  9.7 6.0 %fusion.12 = bf16[512,16]{0,1:T(8,128)(2,1)S(1)} fusion(bf16[1,512,8192]{2,1,0:T(8,128)(2,1)} %param.5, bf16[1,16,8192]{2,1,0:T(8,128)(2,1)} %param.7), kind=kOutput, calls=%fused_computation.10 | convolution fusion | flops 134225920 | bytes 8667136 | tf_op jit(solution)/shard_map/dot_general | solution.py:16
  15.6 0.0 copy-start.3
  15.6 0.9 fusion.15
  16.5 0.0 copy-done.1
  16.6 2.0 fusion.1
  18.6 0.0 all-reduce.3.cloned.1.call-update
  18.6 0.2 all-gather.5.cloned.1.call-start
  18.8 28.9 %all-gather.3.cloned.1.call-done = bf16[1024,1024]{1,0:T(8,128)(2,1)} async-done(((bf16[1024,256]{1,0:T(8,128)(2,1)}), bf16[1024,1024]{1,0:T(8,128)(2,1)}) %all-gather.3.cloned.1.call-update) | async-done | bytes 2097168 | tf_op jit(solution)/shard_map/all_gather | solution.py:15
  47.7 0.0 all-gather.5.cloned.1.call-update
  47.8 0.0 copy-done.3
  47.8 0.5 fusion.23
  48.2 49.4 %all-reduce.3.cloned.1.call-done = (f32[16,8192]{1,0:T(8,128)}, f32[16,1024]{1,0:T(8,128)}) async-done(((f32[16,8192]{1,0:T(8,128)}, f32[16,1024]{1,0:T(8,128)}), (f32[16,8192]{1,0:T(8,128)}, f32[16,1024]{1,0:T(8,128)})) %all-reduce.3.cloned.1.call-update) | async-done | bytes 589840 | tf_op jit(solution)/shard_map/psum | solution.py:41
  97.6 1.5 multiply_bitcast_fusion.1
  99.1 1.9 multiply_bitcast_fusion
  100.9 0.0 copy-start.2
  100.9 149.5 %all-gather.5.cloned.1.call-done = bf16[8192,1024]{1,0:T(8,128)(2,1)} async-done(((bf16[1024,1024]{1,0:T(8,128)(2,1)}), bf16[8192,1024]{1,0:T(8,128)(2,1)}) %all-gather.5.cloned.1.call-update) | async-done | bytes 16777232 | tf_op jit(solution)/shard_map/all_gather | solution.py:24
  250.4 15.8 %fusion.18 = f32[512,8192]{1,0:T(8,128)} fusion(bf16[8192,1024]{1,0:T(8,128)(2,1)} %all-gather.5.cloned.1.call-done, bf16[1,512,1024]{2,1,0:T(8,128)(2,1)S(1)} %copy-done), kind=kOutput, calls=%fused_computation.15 | convolution fusion | flops 8589934592 | bytes 34603008 | tf_op jit(solution)/shard_map/dot_general | solution.py:27
  266.2 0.0 copy-done.2
  266.2 11.5 %fusion = bf16[1,512,8192]{2,1,0:T(8,128)(2,1)} fusion(f32[512,8192]{1,0:T(8,128)} %fusion.18, bf16[512,16]{0,1:T(8,128)(2,1)S(1)} %convolution_convert_fusion, bf16[1,16,8192]{2,1,0:T(8,128)(2,1)S(1)} %copy-done.2), kind=kOutput, calls=%fused_computation.1 | convolution fusion | flops 146800640 | bytes 25444352 | tf_op jit(solution)/shard_map/dot_general | solution.py:36
  277.7 15.5 %fusion.9 = bf16[1,512,1024]{2,1,0:T(8,128)(2,1)} fusion(f32[512,1024]{1,0:T(8,128)S(1)} %fusion.23, bf16[8192,1024]{1,0:T(8,128)(2,1)} %all-gather.5.cloned.1.call-done, bf16[1,512,8192]{2,1,0:T(8,128)(2,1)} %param.5), kind=kOutput, calls=%fused_computation.9 | convolution fusion | flops 8591507456 | bytes 28311552 | tf_op jit(solution)/shard_map/dot_general | solution.py:22
Async XLA Ops:
  7.2 1.2 copy-start
  7.2 40.6 %all-gather.3.cloned.1.call-start = ((), (), s32[]{:S(2)}) async-start(), calls=%async_computation | async-start | bytes 2621440 | tf_op jit(solution)/shard_map/all_gather | solution.py:15
  7.9 89.7 %all-reduce.3.cloned.1.call-start = ((), (), s32[]{:S(2)}) async-start(), calls=%async_computation.2 | async-start | bytes 1179648 | tf_op jit(solution)/shard_map/psum | solution.py:41
  8.4 8.2 %copy-start.1 = (bf16[1,512,8192]{2,1,0:T(8,128)(2,1)S(1)}, bf16[1,512,8192]{2,1,0:T(8,128)(2,1)}, u32[]{:S(2)}) copy-start(bf16[1,512,8192]{2,1,0:T(8,128)(2,1)} %param.5) | copy-start | bytes 25165828
  15.6 32.1 %copy-start.3 = (bf16[1,16,1024]{2,1,0:T(8,128)(2,1)S(1)}, bf16[1,16,1024]{2,1,0:T(8,128)(2,1)}, u32[]{:S(2)}) copy-start(bf16[1,16,1024]{2,1,0:T(8,128)(2,1)} %param.8) | copy-start | bytes 98308
  18.6 231.8 %all-gather.5.cloned.1.call-start = ((), (), s32[]{:S(2)}) async-start(), calls=%async_computation.1 | async-start | bytes 18874368 | tf_op jit(solution)/shard_map/all_gather | solution.py:24
  100.9 165.3 %copy-start.2 = (bf16[1,16,8192]{2,1,0:T(8,128)(2,1)S(1)}, bf16[1,16,8192]{2,1,0:T(8,128)(2,1)}, u32[]{:S(2)}) copy-start(bf16[1,16,8192]{2,1,0:T(8,128)(2,1)} %param.7) | copy-start | bytes 786436
Sparse Core Ops, SparseCore 0:
  9.8 37.8 all-gather.2
  51.3 46.2 all-reduce.2
  99.3 151.0 all-gather.4
where the time goes:
time: 300 us
  waiting for transfers between devices  228 us (76%)
  matrix products  53.4 us (18%)
  between operations  13.8 us (5%)
  other arithmetic  3.34 us (1%)
    all_gather x1, waiting for transfers between devices, body(): lax.all_gather(panel, 'blk', axis=0, tiled=True)  149 us
    psum x1, waiting for transfers between devices, body(): sum_down, sum_up = lax.psum((local_down, local_up), 'seq')  49.4 us
    all_gather x1, waiting for transfers between devices, body(): panel = lax.all_gather(base_weight, 'seq', axis=1, tiled=True)  28.9 us
    dot_general x1, matrix products, body(): lax.dot_general(output_cotangent, lax.all_gather(panel, 'blk', axis=0, ti...  15.8 us
    dot_general x1, matrix products, body(): jnp.dot(token_inputs, lax.all_gather(panel, 'blk', axis=0, tiled=True), p...  15.5 us
    dot_general x1, matrix products, body(): jnp.dot(lowrank_backward, down_matrix, preferred_element_type=jnp.float32)  11.5 us
  transfers between devices with their start and end apart: 3, of which 3 were waited for; matrix products, arithmetic and copies ran while one was open for 5% of the time, Pallas kernels for 0%

commit v1 on v0

--- a/solution.py
+++ b/solution.py
@@ -4,6 +4,19 @@
 from jax.sharding import PartitionSpec as P
 
 adapter_scale = 2.0
+
+
+def collect(x, axis, dim):
+    ways = lax.axis_size(axis)
+    up = [(d, (d + 1) % ways) for d in range(ways)]
+    down = [(d, (d - 1) % ways) for d in range(ways)]
+    earlier, later = ([x], [x])
+    for _ in range(ways // 2):
+        earlier.append(lax.ppermute(earlier[-1], axis, up))
+    for _ in range((ways - 1) // 2):
+        later.append(lax.ppermute(later[-1], axis, down))
+    line = jnp.concatenate([*earlier[::-1], *later[1:]], axis=dim)
+    return jnp.roll(line, (lax.axis_index(axis) - ways // 2) * x.shape[dim], axis=dim)
 
 
 def body(activations, base_weight, adapter_down, adapter_up, cotangent):
@@ -20,9 +33,7 @@
         output_cotangent, up_matrix.T, preferred_element_type=jnp.float32
     ).astype(jnp.bfloat16)
     frozen_keys = jnp.dot(
-        token_inputs,
-        lax.all_gather(panel, "blk", axis=0, tiled=True),
-        preferred_element_type=jnp.float32,
+        token_inputs, collect(panel, "blk", 0), preferred_element_type=jnp.float32
     )
     frozen_gradient = lax.dot_general(
         output_cotangent,

time: 300 us -> 441 us (1.47)
  the two profiles are of different devices: /device:TPU:0 before, /device:TPU:16 now
where the time goes in v1:
time: 441 us; the launch traced here: 440 us
  waiting for transfers between devices  287 us (65%)
  matrix products  57.7 us (13%)
  local copies, waits for them, and re-layouts  48 us (11%)
  starting transfers between devices  30.3 us (7%)
  between operations  13.8 us (3%)
    ppermute x4, waiting for transfers between devices, collect(): earlier.append(lax.ppermute(earlier[-1], axis, up))  240 us
    unnamed x32, local copies, waits for them, and re-layouts  44.9 us
    all_gather x1, waiting for transfers between devices, body(): panel = lax.all_gather(base_weight, 'seq', axis=1, tiled=True)  24.2 us
    ppermute x4, starting transfers between devices, collect(): earlier.append(lax.ppermute(earlier[-1], axis, up))  23.4 us
    ppermute x3, waiting for transfers between devices, collect(): later.append(lax.ppermute(later[-1], axis, down))  22.3 us
    dot_general x1, matrix products, body(): lax.dot_general(output_cotangent, lax.all_gather(panel, 'blk', axis=0, ti...  15.7 us
    dot_general x1, matrix products, body(): jnp.dot(token_inputs, collect(panel, 'blk', 0), preferred_element_type=jn...  15.2 us
    dot_general x1, matrix products, body(): jnp.dot(lowrank_backward, down_matrix, preferred_element_type=jnp.float32)  11.5 us
  transfers between devices with their start and end apart: 10, of which 7 were waited for; matrix products, arithmetic and copies ran while one was open for 18% of the time, Pallas kernels for 0%

profile of v1, /device:TPU:16, one launch (start us, length us, event | category | flops | bytes accessed | tf_op | source)
XLA Modules:
  0.0 439.9 jit_solution(3326842346471647799)
XLA Ops:
  7.2 0.0 all-gather.3.cloned.1.call-start
  7.2 0.7 all-gather.3.cloned.1.call-update
  7.9 0.0 all-reduce.3.cloned.1.call-start
  8.0 0.4 copy-done
  8.4 1.1 convolution_convert_fusion
  9.5 5.7 %fusion.18 = bf16[512,16]{0,1:T(8,128)(2,1)S(1)} fusion(bf16[1,512,8192]{2,1,0:T(8,128)(2,1)} %param.5, bf16[1,16,8192]{2,1,0:T(8,128)(2,1)} %param.7), kind=kOutput, calls=%fused_computation.12 | convolution fusion | flops 134225920 | bytes 8667136 | tf_op jit(solution)/shard_map/dot_general | solution.py:29
  15.2 0.9 fusion.21
  16.1 5.8 %fusion.3 = f32[16,8192]{1,0:T(8,128)} fusion(bf16[512,16]{0,1:T(8,128)(2,1)S(1)} %convolution_convert_fusion, bf16[1,512,8192]{2,1,0:T(8,128)(2,1)} %param.5), kind=kOutput, calls=%fused_computation.4 | convolution fusion | flops 134217728 | bytes 8929280 | tf_op jit(solution)/shard_map/dot_general | solution.py:50
  21.8 0.0 all-reduce.3.cloned.1.call-update
  21.9 0.0 all-gather.5.cloned.1.call-start
  21.9 24.2 %all-gather.3.cloned.1.call-done = bf16[1024,1024]{1,0:T(8,128)(2,1)} async-done(((bf16[1024,256]{1,0:T(8,128)(2,1)}), bf16[1024,1024]{1,0:T(8,128)(2,1)}) %all-gather.3.cloned.1.call-update) | async-done | bytes 2097168 | tf_op jit(solution)/shard_map/all_gather | solution.py:28
  46.1 0.0 all-gather.5.cloned.1.call-update
  46.1 0.1 collective-permute-start
  46.2 25.7 %collective-permute-done = bf16[1024,1024]{1,0:T(8,128)(2,1)S(1)} collective-permute-done((bf16[1024,1024]{1,0:T(8,128)(2,1)}, bf16[1024,1024]{1,0:T(8,128)(2,1)S(1)}, u32[]{:S(2)}, u32[]{:S(2)}) %collective-permute-start) | collective-permute-done | bytes 2097184 | tf_op jit(solution)/shard_map/ppermute | solution.py:15
  71.9 1.4 copy-done.2
  73.2 1.7 collective-permute-start.4
  75.0 58.5 %collective-permute-done.1 = bf16[1024,1024]{1,0:T(8,128)(2,1)S(1)} collective-permute-done((bf16[1024,1024]{1,0:T(8,128)(2,1)S(1)}, bf16[1024,1024]{1,0:T(8,128)(2,1)S(1)}, u32[]{:S(2)}, u32[]{:S(2)}) %collective-permute-start.1) | collective-permute-done | bytes 2097184 | tf_op jit(solution)/shard_map/ppermute | solution.py:15
  133.5 1.3 copy-done.4
  134.8 10.0 %collective-permute-done.4 = bf16[1024,1024]{1,0:T(8,128)(2,1)} collective-permute-done((bf16[1024,1024]{1,0:T(8,128)(2,1)}, bf16[1024,1024]{1,0:T(8,128)(2,1)}, u32[]{:S(2)}, u32[]{:S(2)}) %collective-permute-start.4) | collective-permute-done | bytes 2097184 | tf_op jit(solution)/shard_map/ppermute | solution.py:17
  144.8 2.7 collective-permute-start.5
  147.5 124.4 %collective-permute-done.2 = bf16[1024,1024]{1,0:T(8,128)(2,1)} collective-permute-done((bf16[1024,1024]{1,0:T(8,128)(2,1)S(1)}, bf16[1024,1024]{1,0:T(8,128)(2,1)}, u32[]{:S(2)}, u32[]{:S(2)}) %collective-permute-start.2) | collective-permute-done | bytes 2097184 | tf_op jit(solution)/shard_map/ppermute | solution.py:15
  271.8 23.4 %collective-permute-start.3 = (bf16[1024,1024]{1,0:T(8,128)(2,1)}, bf16[1024,1024]{1,0:T(8,128)(2,1)}, u32[]{:S(2)}, u32[]{:S(2)}) collective-permute-start(bf16[1024,1024]{1,0:T(8,128)(2,1)} %collective-permute-done.2), channel_id=1, source_target_pairs={{0,4},{4,8},{8,12},{12,16},{16,20},{20,24},{24,28},{28,0},{1,5},{5... | collective-permute-start | bytes 6291464 | tf_op jit(solution)/shard_map/ppermute | solution.py:15
  295.2 1.8 fusion.29
  297.0 12.3 %collective-permute-done.5 = bf16[1024,1024]{1,0:T(8,128)(2,1)} collective-permute-done((bf16[1024,1024]{1,0:T(8,128)(2,1)}, bf16[1024,1024]{1,0:T(8,128)(2,1)}, u32[]{:S(2)}, u32[]{:S(2)}) %collective-permute-start.5) | collective-permute-done | bytes 2097184 | tf_op jit(solution)/shard_map/ppermute | solution.py:17
  309.3 2.3 collective-permute-start.6
  311.6 1.9 multiply_bitcast_fusion
  313.5 1.5 multiply_bitcast_fusion.1
  314.9 31.0 %collective-permute-done.3 = bf16[1024,1024]{1,0:T(8,128)(2,1)} collective-permute-done((bf16[1024,1024]{1,0:T(8,128)(2,1)}, bf16[1024,1024]{1,0:T(8,128)(2,1)}, u32[]{:S(2)}, u32[]{:S(2)}) %collective-permute-start.3) | collective-permute-done | bytes 2097184 | tf_op jit(solution)/shard_map/ppermute | solution.py:15
  346.0 3.1 constant_dynamic-update-slice_fusion.15
  349.1 3.1 constant_dynamic-update-slice_fusion.14
  352.1 3.2 constant_dynamic-update-slice_fusion.13
  355.4 3.3 constant_dynamic-update-slice_fusion.12
  358.7 1.6 constant_dynamic-update-slice_fusion.11
  360.2 3.1 constant_dynamic-update-slice_fusion.10
  363.3 3.1 constant_dynamic-update-slice_fusion.9
  366.4 3.1 constant_dynamic-update-slice_fusion.8
  369.5 3.1 constant_dynamic-update-slice_fusion.7
  372.6 3.1 constant_dynamic-update-slice_fusion.6
  375.6 1.5 constant_dynamic-update-slice_fusion.5
  377.2 1.5 constant_dynamic-update-slice_fusion.4
  378.7 1.6 constant_dynamic-update-slice_fusion.3
  380.3 3.1 constant_dynamic-update-slice_fusion.2
  383.4 3.1 constant_dynamic-update-slice_fusion.1
  386.5 3.1 constant_dynamic-update-slice_fusion
  389.5 15.2 %fusion.13 = bf16[1,512,1024]{1,2,0:T(8,128)(2,1)S(1)} fusion(f32[512,1024]{0,1:T(8,128)} %fusion.29, bf16[1,512,8192]{2,1,0:T(8,128)(2,1)} %param.5, bf16[16384,1024]{1,0:T(8,128)(2,1)} %constant_dynamic-update-slice_fusion, s32[]{:T(128)S(6)} %select_n.14), kind=kOutput, calls=%fused_computation.11 | convolution fusion | flops 8591507456 | bytes 28311556 | tf_op jit(solution)/shard_map/dot_general | solution.py:35
  404.8 1.3 copy.10
  406.1 15.7 %fusion.24 = f32[512,8192]{1,0:T(8,128)} fusion(bf16[8192,1024]{1,0:T(8,128)(2,1)} %all-gather.5.cloned.1.call-done, bf16[1,512,1024]{2,1,0:T(8,128)(2,1)S(1)} %copy-done), kind=kOutput, calls=%fused_computation.17 | convolution fusion | flops 8589934592 | bytes 34603008 | tf_op jit(solution)/shard_map/dot_general | solution.py:38
  421.8 11.5 %fusion.2 = bf16[1,512,8192]{2,1,0:T(8,128)(2,1)} fusion(f32[512,8192]{1,0:T(8,128)} %fusion.24, bf16[512,16]{0,1:T(8,128)(2,1)S(1)} %convolution_convert_fusion, bf16[1,16,8192]{2,1,0:T(8,128)(2,1)S(1)} %copy-done.6), kind=kOutput, calls=%fused_computation.3 | convolution fusion | flops 146800640 | bytes 25444352 | tf_op jit(solution)/shard_map/dot_general | solution.py:47
  (18 shorter events, 0.0 us)
Async XLA Ops:
  7.2 1.2 copy-start
  7.2 288.0 %copy-start.7 = (bf16[1,16,1024]{2,1,0:T(8,128)(2,1)S(1)}, bf16[1,16,1024]{2,1,0:T(8,128)(2,1)}, u32[]{:S(2)}) copy-start(bf16[1,16,1024]{2,1,0:T(8,128)(2,1)} %param.8) | copy-start | bytes 98308
  7.2 38.9 %all-gather.3.cloned.1.call-start = ((), (), s32[]{:S(2)}) async-start(), calls=%async_computation | async-start | bytes 2621440 | tf_op jit(solution)/shard_map/all_gather | solution.py:28
  7.9 303.7 %all-reduce.3.cloned.1.call-start = ((), (), s32[]{:S(2)}) async-start(), calls=%async_computation.2 | async-start | bytes 1179648 | tf_op jit(solution)/shard_map/psum | solution.py:52
  21.9 384.2 %all-gather.5.cloned.1.call-start = ((), (), s32[]{:S(2)}) async-start(), calls=%async_computation.1 | async-start | bytes 18874368 | tf_op jit(solution)/shard_map/all_gather | solution.py:40
  46.1 312.5 %copy-start.1 = (bf16[1024,1024]{1,0:T(8,128)(2,1)S(1)}, bf16[1024,1024]{1,0:T(8,128)(2,1)}, u32[]{:S(2)}) copy-start(bf16[1024,1024]{1,0:T(8,128)(2,1)} %all-gather.3.cloned.1.call-done) | copy-start | bytes 6291460
  46.1 25.7 %collective-permute-start = (bf16[1024,1024]{1,0:T(8,128)(2,1)}, bf16[1024,1024]{1,0:T(8,128)(2,1)S(1)}, u32[]{:S(2)}, u32[]{:S(2)}) collective-permute-start(bf16[1024,1024]{1,0:T(8,128)(2,1)} %all-gather.3.cloned.1.call-done), channel_id=1, source_target_pairs={{0,4},{4,8},{8,12},{12,16},{16,20},{20,24},{24,28},{28,0},{1,5},{5... | collective-permute-start | bytes 6291464 | tf_op jit(solution)/shard_map/ppermute | solution.py:15
  71.9 1.4 copy-start.2
  73.2 60.2 %collective-permute-start.1 = (bf16[1024,1024]{1,0:T(8,128)(2,1)S(1)}, bf16[1024,1024]{1,0:T(8,128)(2,1)S(1)}, u32[]{:S(2)}, u32[]{:S(2)}) collective-permute-start(bf16[1024,1024]{1,0:T(8,128)(2,1)S(1)} %collective-permute-done), channel_id=1, source_target_pairs={{0,4},{4,8},{8,12},{12,16},{16,20},{20,24},{24,28},{28,0},{1,5},{5... | collective-permute-start | bytes 6291464 | tf_op jit(solution)/shard_map/ppermute | solution.py:15
  73.2 71.6 %collective-permute-start.4 = (bf16[1024,1024]{1,0:T(8,128)(2,1)}, bf16[1024,1024]{1,0:T(8,128)(2,1)}, u32[]{:S(2)}, u32[]{:S(2)}) collective-permute-start(bf16[1024,1024]{1,0:T(8,128)(2,1)} %all-gather.3.cloned.1.call-done), channel_id=1, source_target_pairs={{0,28},{4,0},{8,4},{12,8},{16,12},{20,16},{24,20},{28,24},{1,29},{... | collective-permute-start | bytes 6291464 | tf_op jit(solution)/shard_map/ppermute | solution.py:17
  133.5 1.3 copy-start.4
  134.8 137.1 %collective-permute-start.2 = (bf16[1024,1024]{1,0:T(8,128)(2,1)S(1)}, bf16[1024,1024]{1,0:T(8,128)(2,1)}, u32[]{:S(2)}, u32[]{:S(2)}) collective-permute-start(bf16[1024,1024]{1,0:T(8,128)(2,1)S(1)} %collective-permute-done.1), channel_id=1, source_target_pairs={{0,4},{4,8},{8,12},{12,16},{16,20},{20,24},{24,28},{28,0},{1,5},{5... | collective-permute-start | bytes 6291464 | tf_op jit(solution)/shard_map/ppermute | solution.py:15
  144.8 164.5 %collective-permute-start.5 = (bf16[1024,1024]{1,0:T(8,128)(2,1)}, bf16[1024,1024]{1,0:T(8,128)(2,1)}, u32[]{:S(2)}, u32[]{:S(2)}) collective-permute-start(bf16[1024,1024]{1,0:T(8,128)(2,1)} %collective-permute-done.4), channel_id=1, source_target_pairs={{0,28},{4,0},{8,4},{12,8},{16,12},{20,16},{24,20},{28,24},{1,29},{... | collective-permute-start | bytes 6291464 | tf_op jit(solution)/shard_map/ppermute | solution.py:17
  271.8 74.1 %collective-permute-start.3 = (bf16[1024,1024]{1,0:T(8,128)(2,1)}, bf16[1024,1024]{1,0:T(8,128)(2,1)}, u32[]{:S(2)}, u32[]{:S(2)}) collective-permute-start(bf16[1024,1024]{1,0:T(8,128)(2,1)} %collective-permute-done.2), channel_id=1, source_target_pairs={{0,4},{4,8},{8,12},{12,16},{16,20},{20,24},{24,28},{28,0},{1,5},{5... | collective-permute-start | bytes 6291464 | tf_op jit(solution)/shard_map/ppermute | solution.py:15
  309.3 57.1 %collective-permute-start.6 = (bf16[1024,1024]{1,0:T(8,128)(2,1)}, bf16[1024,1024]{1,0:T(8,128)(2,1)}, u32[]{:S(2)}, u32[]{:S(2)}) collective-permute-start(bf16[1024,1024]{1,0:T(8,128)(2,1)} %collective-permute-done.5), channel_id=1, source_target_pairs={{0,28},{4,0},{8,4},{12,8},{16,12},{20,16},{24,20},{28,24},{1,29},{... | collective-permute-start | bytes 6291464 | tf_op jit(solution)/shard_map/ppermute | solution.py:17
  352.1 23.5 %copy-start.5 = (bf16[1024,1024]{1,0:T(8,128)(2,1)S(1)}, bf16[1024,1024]{1,0:T(8,128)(2,1)}, u32[]{:S(2)}) copy-start(bf16[1024,1024]{1,0:T(8,128)(2,1)} %copy-done.4) | copy-start | bytes 6291460
  355.4 21.8 %copy-start.3 = (bf16[1024,1024]{1,0:T(8,128)(2,1)S(1)}, bf16[1024,1024]{1,0:T(8,128)(2,1)}, u32[]{:S(2)}) copy-start(bf16[1024,1024]{1,0:T(8,128)(2,1)} %copy-done.2) | copy-start | bytes 6291460
  406.1 15.7 %copy-start.6 = (bf16[1,16,8192]{2,1,0:T(8,128)(2,1)S(1)}, bf16[1,16,8192]{2,1,0:T(8,128)(2,1)}, u32[]{:S(2)}) copy-start(bf16[1,16,8192]{2,1,0:T(8,128)(2,1)} %param.7) | copy-start | bytes 786436
Sparse Core Ops, SparseCore 0:
  9.8 36.2 all-gather.2
  49.7 46.2 all-reduce.2
  97.7 244.7 all-gather.4
